TPU v7x, 512 devices: a whole 4x8x8 slice. The times are simulated.
512 devices in a mesh: row: 16 (over y, z_lo), col: 32 (over z_hi, x, core).
Axes of the slice: x: 4, y: 8, z: 8 (z_hi: 4, z_lo: 2; z = z_hi * 2 + z_lo), core: 2. Of those that a mesh axis runs over, the one named last changes fastest.
Arguments:
- tiles: bfloat16 [16, 32, 32, 256, 256], P('row', 'col'), may hold values from -6 to 6
- tile_ids: int32 [16, 32, 2, 32], P('row', 'col'), may hold values from 0 to 7, as said below
- tile_count: int32 [16, 32], P('row', 'col'), may hold values from 8 to 32
- query_degree: int32 [32768], P('row'), may hold values from 1 to 32
- product_degree: int32 [65536], P('col'), may hold values from 1 to 32
- panel: float32 [64, 65536], P(None, ('col', 'row')), may hold values from -6 to 6
Outputs:
- basis: float32 [64, 65536], P(None, ('col', 'row'))
Inputs may be any that keep to these rules, and one draw needn't show every extreme that they name: `tile_ids`: on each device the 32 (tile row, tile column) pairs are distinct; tile row is below 8 and tile column below 8.
All inputs are finite; a program needn't handle non-finite values.
Results may differ from a plain program's by a relative error of at most 0.0042.
Values may be sent and summed in bfloat16 or wider, within the bound.
A program may use at most 64 MiB of HBM per device.

v0:
```python
import math
import jax
import jax.numpy as jnp
from jax import lax
from jax.sharding import PartitionSpec as P

ITERS = 2
HIGH = lax.Precision.HIGHEST


def orthonormal(lifted, gram):
    lower = jnp.linalg.cholesky(gram)
    return lax.linalg.triangular_solve(lower, lifted, left_side=True, lower=True)


def shards(tiles, tile_ids, tile_count, query_degree, product_degree, panel):
    tile_set = tiles[0, 0]
    slot_ids = tile_ids[0, 0]
    live_count = tile_count[0, 0]
    slots = tile_set.shape[0]
    side = tile_set.shape[1]
    width = panel.shape[0]
    query_tiles = query_degree.shape[0] // side
    product_tiles = product_degree.shape[0] // side
    live_slot = (jnp.arange(slots, dtype=jnp.int32) < live_count).astype(jnp.float32)
    row_hot = (slot_ids[0][:, None] == jnp.arange(query_tiles, dtype=jnp.int32)[None, :]).astype(
        jnp.float32
    ) * live_slot[:, None]
    col_hot = (slot_ids[1][:, None] == jnp.arange(product_tiles, dtype=jnp.int32)[None, :]).astype(
        jnp.float32
    ) * live_slot[:, None]
    qscale = 1.0 / jnp.sqrt(query_degree.astype(jnp.float32))
    pscale = 1.0 / jnp.sqrt(product_degree.astype(jnp.float32))
    row_at = lax.axis_index("row")
    col_at = lax.axis_index("col")
    share = panel.shape[1]
    my_pscale = lax.dynamic_slice_in_dim(pscale, row_at * share, share)
    root_count = math.sqrt(product_degree.shape[0] * lax.axis_size("col"))
    current = panel
    for iteration in range(ITERS):
        scaled = (current * my_pscale[None, :]).astype(jnp.bfloat16)
        scaled_block = lax.all_gather(scaled, "row", axis=1, tiled=True)
        picked = jnp.take(scaled_block.reshape(width, product_tiles, side), slot_ids[1], axis=1)
        products = jnp.einsum("rkj,kij->kri", picked, tile_set, preferred_element_type=jnp.float32)
        partial_sum = jnp.einsum("kq,kri->rqi", row_hot, products, precision=HIGH).reshape(
            width, query_tiles * side
        )
        query_share = lax.psum_scatter(partial_sum, "col", scatter_dimension=1, tiled=True)
        columns = query_share.shape[1]
        my_qscale = lax.dynamic_slice_in_dim(qscale, col_at * columns, columns)
        rounded = (query_share * my_qscale[None, :]).astype(jnp.bfloat16)
        query_block = lax.all_gather(rounded, "col", axis=1, tiled=True)
        backward_picked = jnp.take(
            query_block.reshape(width, query_tiles, side), slot_ids[0], axis=1
        )
        backward_products = jnp.einsum(
            "rki,kij->krj", backward_picked, tile_set, preferred_element_type=jnp.float32
        )
        lifted = (
            lax.psum_scatter(
                jnp.einsum("kp,krj->rpj", col_hot, backward_products, precision=HIGH).reshape(
                    width, product_tiles * side
                ),
                "row",
                scatter_dimension=1,
                tiled=True,
            )
            * my_pscale[None, :]
        )
        gram = lax.psum(jnp.einsum("ri,si->rs", lifted, lifted, precision=HIGH), ("row", "col"))
        current = orthonormal(lifted, gram)
    return current * root_count


def solution(mesh):
    in_specs = (
        P("row", "col", None, None, None),
        P("row", "col", None, None),
        P("row", "col"),
        P("row"),
        P("col"),
        P(None, ("col", "row")),
    )
    out_specs = P(None, ("col", "row"))
    return jax.shard_map(shards, mesh=mesh, in_specs=in_specs, out_specs=out_specs, check_vma=False)
```

profile of v0, /device:TPU:24, one launch (start us, length us, event | category | flops | bytes accessed | tf_op | source)
XLA Modules:
  0.0 757.7 jit_solution(1532699937566994767)
XLA Ops:
  6.5 0.0 reduce-scatter.13.cloned.1.call-start
  6.5 0.8 slice_bitcast_fusion.1
  7.3 0.8 compare_and_fusion
  8.7 0.8 fusion.78
  9.5 0.8 multiply_convert_fusion.2
  10.3 32.3 %all_gather.12 = bf16[64,2048]{1,0:T(8,128)(2,1)S(1)} all-gather(bf16[64,128]{1,0:T(8,128)(2,1)S(1)} %multiply_convert_fusion.2), channel_id=1, replica_groups=mesh['row'=16,'col'=32] {'row'}, dimensions={1}, use_global_device_ids=true | all-gather | bytes 278528 | tf_op jit(solution)/shard_map/all_gather | solution.py:42
  42.6 0.6 gather_fusion
  43.2 3.6 fusion.6
  46.8 2.4 fusion.16
  49.1 1.4 copy.55
  50.5 0.0 reduce-scatter.13.cloned.1.call-update
  50.5 0.0 reduce-scatter.9.cloned.1.call-start
  50.6 0.8 fusion.77
  51.3 101.7 %reduce-scatter.13.cloned.1.call-done = f32[64,64]{1,0:T(8,128)} async-done(((f32[2048,64]{1,0:T(8,128)}), f32[64,64]{1,0:T(8,128)}) %reduce-scatter.13.cloned.1.call-update) | async-done | bytes 16400
  153.1 0.8 copy.52
  153.9 0.1 copy.31
  154.0 43.8 %all_gather.13 = bf16[64,2048]{0,1:T(8,128)(2,1)S(1)} all-gather(bf16[64,64]{0,1:T(8,128)(2,1)S(1)} %copy.31), channel_id=1, replica_groups=mesh['row'=16,'col'=32] {'col'}, dimensions={1}, use_global_device_ids=true | all-gather | bytes 270336 | tf_op jit(solution)/shard_map/all_gather | solution.py:52
  197.8 0.2 copy.33
  198.0 0.6 gather_fusion.1
  198.6 3.1 fusion.4
  201.7 2.4 fusion.12
  204.1 1.0 copy.59
  205.0 0.0 reduce-scatter.9.cloned.1.call-update
  205.0 0.0 reduce-scatter.15.cloned.1.call-start
  205.1 67.3 %reduce-scatter.9.cloned.1.call-done = f32[64,128]{1,0:T(8,128)} async-done(((f32[64,2048]{1,0:T(8,128)}), f32[64,128]{1,0:T(8,128)}) %reduce-scatter.9.cloned.1.call-update) | async-done | bytes 32784 | tf_op jit(solution)/shard_map/reduce_scatter | solution.py:60
  272.4 1.0 fusion.51
  273.4 98.9 %psum.14 = f32[64,64]{0,1:T(8,128)S(1)} all-reduce(f32[64,64]{0,1:T(8,128)S(1)} %fusion.51), channel_id=1, replica_groups=mesh['row'=16,'col'=32] {'row','col'}, use_global_device_ids=true, to_apply=%region_2.4 | all-reduce | flops 4096 | bytes 32768 | tf_op jit(solution)/shard_map/psum | solution.py:70
  372.4 0.1 copy.36
  372.5 5.8 cholesky.44
  378.3 0.6 compare_reduce_fusion.1
  379.0 0.7 fusion.39
  379.6 4.9 custom-call.6
  384.5 1.0 fusion.22
  385.6 29.2 %all_gather.14 = bf16[64,2048]{1,0:T(8,128)(2,1)S(1)} all-gather(bf16[64,128]{1,0:T(8,128)(2,1)S(1)} %fusion.22), channel_id=1, replica_groups=mesh['row'=16,'col'=32] {'row'}, dimensions={1}, use_global_device_ids=true | all-gather | bytes 278528 | tf_op jit(solution)/shard_map/all_gather | solution.py:42
  414.8 0.6 gather_fusion.2
  415.4 3.6 fusion.2
  419.0 2.4 fusion.19
  421.4 1.4 copy.56
  422.7 0.0 reduce-scatter.15.cloned.1.call-update
  422.8 0.0 reduce-scatter.11.cloned.1.call-start
  422.8 95.3 %reduce-scatter.15.cloned.1.call-done = f32[64,64]{1,0:T(8,128)} async-done(((f32[2048,64]{1,0:T(8,128)}), f32[64,64]{1,0:T(8,128)}) %reduce-scatter.15.cloned.1.call-update) | async-done | bytes 16400
  518.1 0.8 copy.54
  518.9 0.1 copy.39
  519.0 43.8 %all_gather.15 = bf16[64,2048]{0,1:T(8,128)(2,1)S(1)} all-gather(bf16[64,64]{0,1:T(8,128)(2,1)S(1)} %copy.39), channel_id=1, replica_groups=mesh['row'=16,'col'=32] {'col'}, dimensions={1}, use_global_device_ids=true | all-gather | bytes 270336 | tf_op jit(solution)/shard_map/all_gather | solution.py:52
  562.8 0.2 copy.41
  563.0 0.6 gather_fusion.3
  563.6 3.1 fusion
  566.7 2.4 fusion.8
  569.1 1.0 copy.60
  570.0 0.0 reduce-scatter.11.cloned.1.call-update
  570.1 67.3 %reduce-scatter.11.cloned.1.call-done = f32[64,128]{1,0:T(8,128)} async-done(((f32[64,2048]{1,0:T(8,128)}), f32[64,128]{1,0:T(8,128)}) %reduce-scatter.11.cloned.1.call-update) | async-done | bytes 32784 | tf_op jit(solution)/shard_map/reduce_scatter | solution.py:60
  637.4 1.0 fusion.48
  638.4 99.0 %psum.15 = f32[64,64]{0,1:T(8,128)S(1)} all-reduce(f32[64,64]{0,1:T(8,128)S(1)} %fusion.48), channel_id=1, replica_groups=mesh['row'=16,'col'=32] {'row','col'}, use_global_device_ids=true, to_apply=%region_7.11 | all-reduce | flops 4096 | bytes 32768 | tf_op jit(solution)/shard_map/psum | solution.py:70
  737.4 0.1 copy.44
  737.5 5.8 cholesky.55
  743.4 0.6 compare_reduce_fusion
  744.0 0.7 fusion.40
  744.7 4.9 custom-call.7
  749.6 1.6 convolution_multiply_fusion
  (11 shorter events, 0.1 us)
Async XLA Ops:
  6.5 146.5 %reduce-scatter.13.cloned.1.call-start = ((), (), s32[]{:S(2)}) async-start(), calls=%async_computation.6 | async-start | bytes 1081344
  50.5 221.9 %reduce-scatter.9.cloned.1.call-start = ((), (), s32[]{:S(2)}) async-start(), calls=%async_computation.4 | async-start | bytes 557056 | tf_op jit(solution)/shard_map/reduce_scatter | solution.py:60
  205.0 313.1 %reduce-scatter.15.cloned.1.call-start = ((), (), s32[]{:S(2)}) async-start(), calls=%async_computation.7 | async-start | bytes 1081344
  422.8 214.6 %reduce-scatter.11.cloned.1.call-start = ((), (), s32[]{:S(2)}) async-start(), calls=%async_computation.5 | async-start | bytes 557056 | tf_op jit(solution)/shard_map/reduce_scatter | solution.py:60
Sparse Core Ops, SparseCore 0:
  50.6 102.3 reduce-scatter.12
  205.2 67.2 reduce-scatter.8
  422.9 95.1 reduce-scatter.14
  570.2 67.1 reduce-scatter.10
where the time goes:
time: 759 us; the launch traced here: 758 us
  blocking collectives  347 us (46%)
  waiting for transfers between devices  332 us (44%)
  matrix products  27.4 us (4%)
  other arithmetic  27.3 us (4%)
  between operations  14 us (2%)
  local copies, waits for them, and re-layouts  10.3 us (1%)
    psum x2, blocking collectives, shards(): lax.psum(jnp.einsum('ri,si->rs', lifted, lifted, precision=HIGH), ('row',...  198 us
    unnamed x6, waiting for transfers between devices  197 us
    reduce_scatter x2, waiting for transfers between devices, shards(): lax.psum_scatter(jnp.einsum('kp,krj->rpj', col_hot, backward_products, pr...  135 us
    all_gather x2, blocking collectives, shards(): query_block = lax.all_gather(rounded, 'col', axis=1, tiled=True)  87.6 us
    all_gather x2, blocking collectives, shards(): scaled_block = lax.all_gather(scaled, 'row', axis=1, tiled=True)  61.5 us
  transfers between devices with their start and end apart: 4, of which 4 were waited for; matrix products, arithmetic and copies ran while one was open for 0% of the time, Pallas kernels for 0%

commit v1 on v0

--- a/solution.py
+++ b/solution.py
@@ -67,7 +67,9 @@
             )
             * my_pscale[None, :]
         )
-        gram = lax.psum(jnp.einsum("ri,si->rs", lifted, lifted, precision=HIGH), ("row", "col"))
+        gram = jnp.einsum("ri,si->rs", lifted, lifted, precision=HIGH)
+        for h in ("col", "row"):
+            gram = lax.psum(gram, axis_name=h)
         current = orthonormal(lifted, gram)
     return current * root_count
 

time: 759 us -> 966 us (1.27)
  the two profiles are of different devices: /device:TPU:24 before, /device:TPU:32 now
where the time goes in v1:
time: 966 us; the launch traced here: 965 us
  blocking collectives  554 us (57%)
  waiting for transfers between devices  332 us (34%)
  matrix products  27.4 us (3%)
  other arithmetic  27.3 us (3%)
  between operations  14 us (1%)
  local copies, waits for them, and re-layouts  10.3 us (1%)
    psum x4, blocking collectives, shards(): gram = lax.psum(gram, axis_name=h)  402 us
    unnamed x6, waiting for transfers between devices  197 us
    reduce_scatter x2, waiting for transfers between devices, shards(): lax.psum_scatter(jnp.einsum('kp,krj->rpj', col_hot, backward_products, pr...  135 us
    all_gather x2, blocking collectives, shards(): query_block = lax.all_gather(rounded, 'col', axis=1, tiled=True)  87.6 us
    all_gather x2, blocking collectives, shards(): scaled_block = lax.all_gather(scaled, 'row', axis=1, tiled=True)  64.5 us
  transfers between devices with their start and end apart: 4, of which 4 were waited for; matrix products, arithmetic and copies ran while one was open for 0% of the time, Pallas kernels for 0%

profile of v1, /device:TPU:32, one launch (start us, length us, event | category | flops | bytes accessed | tf_op | source)
XLA Modules:
  0.0 965.3 jit_solution(204942643055748337)
XLA Ops:
  6.5 0.0 reduce-scatter.13.cloned.1.call-start
  6.5 0.8 slice_bitcast_fusion.1
  7.3 0.8 compare_and_fusion
  8.7 0.8 fusion.78
  9.5 0.8 multiply_convert_fusion.2
  10.3 33.4 %all_gather.12 = bf16[64,2048]{1,0:T(8,128)(2,1)S(1)} all-gather(bf16[64,128]{1,0:T(8,128)(2,1)S(1)} %multiply_convert_fusion.2), channel_id=1, replica_groups=mesh['row'=16,'col'=32] {'row'}, dimensions={1}, use_global_device_ids=true | all-gather | bytes 278528 | tf_op jit(solution)/shard_map/all_gather | solution.py:42
  43.7 0.6 gather_fusion
  44.3 3.6 fusion.6
  47.9 2.4 fusion.16
  50.2 1.4 copy.55
  51.6 0.0 reduce-scatter.13.cloned.1.call-update
  51.6 0.0 reduce-scatter.9.cloned.1.call-start
  51.7 0.8 fusion.77
  52.4 100.5 %reduce-scatter.13.cloned.1.call-done = f32[64,64]{1,0:T(8,128)} async-done(((f32[2048,64]{1,0:T(8,128)}), f32[64,64]{1,0:T(8,128)}) %reduce-scatter.13.cloned.1.call-update) | async-done | bytes 16400
  153.0 0.8 copy.52
  153.8 0.1 copy.31
  153.9 43.8 %all_gather.13 = bf16[64,2048]{0,1:T(8,128)(2,1)S(1)} all-gather(bf16[64,64]{0,1:T(8,128)(2,1)S(1)} %copy.31), channel_id=1, replica_groups=mesh['row'=16,'col'=32] {'col'}, dimensions={1}, use_global_device_ids=true | all-gather | bytes 270336 | tf_op jit(solution)/shard_map/all_gather | solution.py:52
  197.7 0.2 copy.33
  197.9 0.6 gather_fusion.1
  198.5 3.1 fusion.4
  201.6 2.4 fusion.12
  203.9 1.0 copy.59
  204.9 0.0 reduce-scatter.9.cloned.1.call-update
  204.9 0.0 reduce-scatter.15.cloned.1.call-start
  205.0 67.3 %reduce-scatter.9.cloned.1.call-done = f32[64,128]{1,0:T(8,128)} async-done(((f32[64,2048]{1,0:T(8,128)}), f32[64,128]{1,0:T(8,128)}) %reduce-scatter.9.cloned.1.call-update) | async-done | bytes 32784 | tf_op jit(solution)/shard_map/reduce_scatter | solution.py:60
  272.3 1.0 fusion.51
  273.3 138.2 %psum.28 = f32[64,64]{0,1:T(8,128)S(1)} all-reduce(f32[64,64]{0,1:T(8,128)S(1)} %fusion.51), channel_id=1, replica_groups=mesh['row'=16,'col'=32] {'col'}, use_global_device_ids=true, to_apply=%region_2.4 | all-reduce | flops 4096 | bytes 32768 | tf_op jit(solution)/shard_map/psum | solution.py:72
  411.5 63.0 %psum.29 = f32[64,64]{0,1:T(8,128)S(1)} all-reduce(f32[64,64]{0,1:T(8,128)S(1)} %psum.28), channel_id=1, replica_groups=mesh['row'=16,'col'=32] {'row'}, use_global_device_ids=true, to_apply=%region_3.5 | all-reduce | flops 4096 | bytes 32768 | tf_op jit(solution)/shard_map/psum | solution.py:72
  474.5 0.1 copy.36
  474.6 5.8 cholesky.44
  480.5 0.6 compare_reduce_fusion.1
  481.1 0.7 fusion.39
  481.8 4.9 custom-call.6
  486.7 1.0 fusion.22
  487.7 31.1 %all_gather.14 = bf16[64,2048]{1,0:T(8,128)(2,1)S(1)} all-gather(bf16[64,128]{1,0:T(8,128)(2,1)S(1)} %fusion.22), channel_id=1, replica_groups=mesh['row'=16,'col'=32] {'row'}, dimensions={1}, use_global_device_ids=true | all-gather | bytes 278528 | tf_op jit(solution)/shard_map/all_gather | solution.py:42
  518.8 0.6 gather_fusion.2
  519.4 3.6 fusion.2
  523.0 2.4 fusion.19
  525.4 1.4 copy.56
  526.8 0.0 reduce-scatter.15.cloned.1.call-update
  526.8 0.0 reduce-scatter.11.cloned.1.call-start
  526.8 96.5 %reduce-scatter.15.cloned.1.call-done = f32[64,64]{1,0:T(8,128)} async-done(((f32[2048,64]{1,0:T(8,128)}), f32[64,64]{1,0:T(8,128)}) %reduce-scatter.15.cloned.1.call-update) | async-done | bytes 16400
  623.3 0.8 copy.54
  624.2 0.1 copy.39
  624.3 43.8 %all_gather.15 = bf16[64,2048]{0,1:T(8,128)(2,1)S(1)} all-gather(bf16[64,64]{0,1:T(8,128)(2,1)S(1)} %copy.39), channel_id=1, replica_groups=mesh['row'=16,'col'=32] {'col'}, dimensions={1}, use_global_device_ids=true | all-gather | bytes 270336 | tf_op jit(solution)/shard_map/all_gather | solution.py:52
  668.1 0.2 copy.41
  668.3 0.6 gather_fusion.3
  668.9 3.1 fusion
  672.0 2.4 fusion.8
  674.3 1.0 copy.60
  675.3 0.0 reduce-scatter.11.cloned.1.call-update
  675.3 67.4 %reduce-scatter.11.cloned.1.call-done = f32[64,128]{1,0:T(8,128)} async-done(((f32[64,2048]{1,0:T(8,128)}), f32[64,128]{1,0:T(8,128)}) %reduce-scatter.11.cloned.1.call-update) | async-done | bytes 32784 | tf_op jit(solution)/shard_map/reduce_scatter | solution.py:60
  742.7 1.0 fusion.48
  743.8 138.2 %psum.30 = f32[64,64]{0,1:T(8,128)S(1)} all-reduce(f32[64,64]{0,1:T(8,128)S(1)} %fusion.48), channel_id=1, replica_groups=mesh['row'=16,'col'=32] {'col'}, use_global_device_ids=true, to_apply=%region_8.0 | all-reduce | flops 4096 | bytes 32768 | tf_op jit(solution)/shard_map/psum | solution.py:72
  881.9 63.0 %psum.31 = f32[64,64]{0,1:T(8,128)S(1)} all-reduce(f32[64,64]{0,1:T(8,128)S(1)} %psum.30), channel_id=1, replica_groups=mesh['row'=16,'col'=32] {'row'}, use_global_device_ids=true, to_apply=%region_9.13 | all-reduce | flops 4096 | bytes 32768 | tf_op jit(solution)/shard_map/psum | solution.py:72
  945.0 0.1 copy.44
  945.1 5.8 cholesky.55
  950.9 0.6 compare_reduce_fusion
  951.6 0.7 fusion.40
  952.2 4.9 custom-call.7
  957.1 1.6 convolution_multiply_fusion
  (11 shorter events, 0.1 us)
Async XLA Ops:
  6.5 146.4 %reduce-scatter.13.cloned.1.call-start = ((), (), s32[]{:S(2)}) async-start(), calls=%async_computation.6 | async-start | bytes 1081344
  51.6 220.7 %reduce-scatter.9.cloned.1.call-start = ((), (), s32[]{:S(2)}) async-start(), calls=%async_computation.4 | async-start | bytes 557056 | tf_op jit(solution)/shard_map/reduce_scatter | solution.py:60
  204.9 418.4 %reduce-scatter.15.cloned.1.call-start = ((), (), s32[]{:S(2)}) async-start(), calls=%async_computation.7 | async-start | bytes 1081344
  526.8 216.0 %reduce-scatter.11.cloned.1.call-start = ((), (), s32[]{:S(2)}) async-start(), calls=%async_computation.5 | async-start | bytes 557056 | tf_op jit(solution)/shard_map/reduce_scatter | solution.py:60
Sparse Core Ops, SparseCore 0:
  51.7 101.1 reduce-scatter.12
  205.0 67.1 reduce-scatter.8
  526.9 96.3 reduce-scatter.14
  675.4 67.2 reduce-scatter.10

commit v2 on v0

--- a/solution.py
+++ b/solution.py
@@ -39,7 +39,13 @@
     current = panel
     for iteration in range(ITERS):
         scaled = (current * my_pscale[None, :]).astype(jnp.bfloat16)
-        scaled_block = lax.all_gather(scaled, "row", axis=1, tiled=True)
+        update_the_forms = lambda sample, axis_tag: jnp.concatenate(
+            lax.all_to_all(
+                jnp.stack([sample for _ in range(lax.axis_size(axis_tag))]), axis_tag, 0, 0
+            ),
+            axis=1,
+        )
+        scaled_block = update_the_forms(scaled, "row")
         picked = jnp.take(scaled_block.reshape(width, product_tiles, side), slot_ids[1], axis=1)
         products = jnp.einsum("rkj,kij->kri", picked, tile_set, preferred_element_type=jnp.float32)
         partial_sum = jnp.einsum("kq,kri->rqi", row_hot, products, precision=HIGH).reshape(

time: 759 us -> 724 us (0.954)
  blocking collectives: 347 us -> 301 us
  starting transfers between devices: 0.13 us -> 9.31 us
    all_gather x2 -> x0, blocking collectives: 61.5 us -> none  [shards(): scaled_block = lax.all_gather(scaled, 'row', axis=1, tiled=True)]
    all_to_all x0 -> x1, blocking collectives: none -> 15.3 us  [shards(): lax.all_to_all(jnp.stack([sample for _ in range(lax.axis_size(axis_tag))]...]
    all_to_all x0 -> x1, starting transfers between devices: none -> 9.15 us  [shards(): lax.all_to_all(jnp.stack([sample for _ in range(lax.axis_size(axis_tag))]...]
  transfers between devices with their start and end apart: 4 -> 5, of which waited for: 4 -> 5; matrix products, arithmetic and copies ran while one was open for 0% -> 0% of each run, Pallas kernels for 0% -> 0%
where the time goes in v2:
time: 724 us; the launch traced here: 723 us
  waiting for transfers between devices  333 us (46%)
  blocking collectives  301 us (42%)
  matrix products  27.4 us (4%)
  other arithmetic  27.2 us (4%)
  between operations  14 us (2%)
  local copies, waits for them, and re-layouts  11.6 us (2%)
  starting transfers between devices  9.31 us (1%)
    psum x2, blocking collectives, shards(): lax.psum(jnp.einsum('ri,si->rs', lifted, lifted, precision=HIGH), ('row',...  198 us
    unnamed x6, waiting for transfers between devices  190 us
    reduce_scatter x2, waiting for transfers between devices, shards(): lax.psum_scatter(jnp.einsum('kp,krj->rpj', col_hot, backward_products, pr...  135 us
    all_gather x2, blocking collectives, shards(): query_block = lax.all_gather(rounded, 'col', axis=1, tiled=True)  87.7 us
    all_to_all x1, blocking collectives, shards(): lax.all_to_all(jnp.stack([sample for _ in range(lax.axis_size(axis_tag))]...  15.3 us
  transfers between devices with their start and end apart: 5, of which 5 were waited for; matrix products, arithmetic and copies ran while one was open for 0% of the time, Pallas kernels for 0%

profile of v2, /device:TPU:24, one launch (start us, length us, event | category | flops | bytes accessed | tf_op | source)
XLA Modules:
  0.0 723.2 jit_solution(14288274045298849954)
XLA Ops:
  6.5 0.8 fusion.78
  7.3 0.8 multiply_convert_fusion.2
  8.1 0.7 stack.4
  8.8 9.1 %all-to-all-start = ((bf16[16,64,128]{2,1,0:T(8,128)(2,1)}), bf16[16,64,128]{2,1,0:T(8,128)(2,1)S(1)}, u32[]{:S(2)}, u32[]{:S(2)}) async-start(bf16[16,64,128]{2,1,0:T(8,128)(2,1)} %stack.4), calls=%async_computation | async-start | bytes 524288 | tf_op jit(solution)/shard_map/all_to_all | solution.py:43
  18.0 0.0 reduce-scatter.13.cloned.1.call-start
  18.0 0.8 compare_and_fusion
  19.4 0.8 slice_bitcast_fusion.1
  20.2 7.3 %all-to-all-done = bf16[16,64,128]{2,1,0:T(8,128)(2,1)S(1)} async-done(((bf16[16,64,128]{2,1,0:T(8,128)(2,1)}), bf16[16,64,128]{2,1,0:T(8,128)(2,1)S(1)}, u32[]{:S(2)}, u32[]{:S(2)}) %all-to-all-start) | async-done | bytes 262176 | tf_op jit(solution)/shard_map/all_to_all | solution.py:43
  27.5 0.2 copy.29
  27.7 0.1 reshape_reshape.6
  27.8 0.6 gather_fusion
  28.4 3.6 fusion.6
  32.0 2.4 fusion.16
  34.4 1.4 copy.57
  35.7 0.0 reduce-scatter.13.cloned.1.call-update
  35.8 0.0 reduce-scatter.9.cloned.1.call-start
  35.8 0.8 fusion.77
  36.6 98.5 %reduce-scatter.13.cloned.1.call-done = f32[64,64]{1,0:T(8,128)} async-done(((f32[2048,64]{1,0:T(8,128)}), f32[64,64]{1,0:T(8,128)}) %reduce-scatter.13.cloned.1.call-update) | async-done | bytes 16400
  135.0 0.8 copy.54
  135.9 0.1 copy.32
  136.0 43.8 %all_gather.6 = bf16[64,2048]{0,1:T(8,128)(2,1)S(1)} all-gather(bf16[64,64]{0,1:T(8,128)(2,1)S(1)} %copy.32), channel_id=1, replica_groups=mesh['row'=16,'col'=32] {'col'}, dimensions={1}, use_global_device_ids=true | all-gather | bytes 270336 | tf_op jit(solution)/shard_map/all_gather | solution.py:58
  179.8 0.2 copy.34
  180.0 0.6 gather_fusion.1
  180.6 3.1 fusion.4
  183.7 2.4 fusion.12
  186.1 1.0 copy.59
  187.0 0.0 reduce-scatter.9.cloned.1.call-update
  187.0 0.0 reduce-scatter.15.cloned.1.call-start
  187.1 67.5 %reduce-scatter.9.cloned.1.call-done = f32[64,128]{1,0:T(8,128)} async-done(((f32[64,2048]{1,0:T(8,128)}), f32[64,128]{1,0:T(8,128)}) %reduce-scatter.9.cloned.1.call-update) | async-done | bytes 32784 | tf_op jit(solution)/shard_map/reduce_scatter | solution.py:66
  254.6 1.0 fusion.51
  255.6 99.0 %psum.14 = f32[64,64]{0,1:T(8,128)S(1)} all-reduce(f32[64,64]{0,1:T(8,128)S(1)} %fusion.51), channel_id=1, replica_groups=mesh['row'=16,'col'=32] {'row','col'}, use_global_device_ids=true, to_apply=%region_2.4 | all-reduce | flops 4096 | bytes 32768 | tf_op jit(solution)/shard_map/psum | solution.py:76
  354.7 0.1 copy.37
  354.7 5.8 cholesky.44
  360.6 0.6 compare_reduce_fusion.1
  361.3 0.7 fusion.39
  361.9 4.9 custom-call.6
  366.8 1.0 fusion.22
  367.9 15.3 %all_to_all.10 = bf16[16,64,128]{2,1,0:T(8,128)(2,1)S(1)} all-to-all(bf16[16,64,128]{2,1,0:T(8,128)(2,1)S(1)} %stack.5), channel_id=1, replica_groups=mesh['row'=16,'col'=32] {'row'}, dimensions={0} | all-to-all | bytes 524288 | tf_op jit(solution)/shard_map/all_to_all | solution.py:43
  383.2 0.2 copy.38
  383.4 0.1 reshape_reshape.7
  383.6 0.6 gather_fusion.2
  384.2 3.6 fusion.2
  387.8 2.4 fusion.19
  390.1 1.4 copy.58
  391.5 0.0 reduce-scatter.15.cloned.1.call-update
  391.5 0.0 reduce-scatter.11.cloned.1.call-start
  391.6 91.9 %reduce-scatter.15.cloned.1.call-done = f32[64,64]{1,0:T(8,128)} async-done(((f32[2048,64]{1,0:T(8,128)}), f32[64,64]{1,0:T(8,128)}) %reduce-scatter.15.cloned.1.call-update) | async-done | bytes 16400
  483.4 0.8 copy.56
  484.3 0.1 copy.41
  484.4 43.8 %all_gather.7 = bf16[64,2048]{0,1:T(8,128)(2,1)S(1)} all-gather(bf16[64,64]{0,1:T(8,128)(2,1)S(1)} %copy.41), channel_id=1, replica_groups=mesh['row'=16,'col'=32] {'col'}, dimensions={1}, use_global_device_ids=true | all-gather | bytes 270336 | tf_op jit(solution)/shard_map/all_gather | solution.py:58
  528.2 0.2 copy.43
  528.4 0.6 gather_fusion.3
  529.0 3.1 fusion
  532.1 2.4 fusion.8
  534.5 1.0 copy.60
  535.4 67.3 %reduce-scatter.11.cloned.1.call-done = f32[64,128]{1,0:T(8,128)} async-done(((f32[64,2048]{1,0:T(8,128)}), f32[64,128]{1,0:T(8,128)}) %reduce-scatter.11.cloned.1.call-update) | async-done | bytes 32784 | tf_op jit(solution)/shard_map/reduce_scatter | solution.py:66
  602.8 1.0 fusion.48
  603.8 99.1 %psum.15 = f32[64,64]{0,1:T(8,128)S(1)} all-reduce(f32[64,64]{0,1:T(8,128)S(1)} %fusion.48), channel_id=1, replica_groups=mesh['row'=16,'col'=32] {'row','col'}, use_global_device_ids=true, to_apply=%region_7.11 | all-reduce | flops 4096 | bytes 32768 | tf_op jit(solution)/shard_map/psum | solution.py:76
  702.9 0.1 copy.46
  703.0 5.8 cholesky.55
  708.8 0.6 compare_reduce_fusion
  709.5 0.7 fusion.40
  710.2 4.9 custom-call.7
  715.0 1.6 convolution_multiply_fusion
  (13 shorter events, 0.3 us)
Async XLA Ops:
  8.8 18.7 %all-to-all-start = ((bf16[16,64,128]{2,1,0:T(8,128)(2,1)}), bf16[16,64,128]{2,1,0:T(8,128)(2,1)S(1)}, u32[]{:S(2)}, u32[]{:S(2)}) async-start(bf16[16,64,128]{2,1,0:T(8,128)(2,1)} %stack.4), calls=%async_computation | async-start | bytes 524288 | tf_op jit(solution)/shard_map/all_to_all | solution.py:43
  18.0 117.1 %reduce-scatter.13.cloned.1.call-start = ((), (), s32[]{:S(2)}) async-start(), calls=%async_computation.8 | async-start | bytes 1081344
  35.8 218.8 %reduce-scatter.9.cloned.1.call-start = ((), (), s32[]{:S(2)}) async-start(), calls=%async_computation.6 | async-start | bytes 557056 | tf_op jit(solution)/shard_map/reduce_scatter | solution.py:66
  187.0 296.4 %reduce-scatter.15.cloned.1.call-start = ((), (), s32[]{:S(2)}) async-start(), calls=%async_computation.9 | async-start | bytes 1081344
  391.5 211.3 %reduce-scatter.11.cloned.1.call-start = ((), (), s32[]{:S(2)}) async-start(), calls=%async_computation.7 | async-start | bytes 557056 | tf_op jit(solution)/shard_map/reduce_scatter | solution.py:66
Sparse Core Ops, SparseCore 0:
  35.9 99.1 reduce-scatter.12
  187.2 67.3 reduce-scatter.8
  391.6 91.7 reduce-scatter.14
  535.6 67.1 reduce-scatter.10
